TPU v7x, 256 devices: a whole 4x4x8 slice. The times are simulated.
256 devices in a mesh: row: 32 (over y, z), col: 8 (over x, core).
Axes of the slice: x: 4, y: 4, z: 8, core: 2. Of those that a mesh axis runs over, the one named last changes fastest.
Arguments:
- trail_adjoint: float32 [24576, 24576], P('row', 'col'), may hold values from -3 to 3
- panel: float32 [24576, 256], P(('row', 'col')), may hold values from -0.0390625 to 0.0390625
- panel_adjoint: float32 [24576, 256], P(('row', 'col')), may hold values from -6 to 6
- diag_factor: float32 [256, 256], replicated, as said below
- diag_inverse: float32 [256, 256], replicated, as said below
- diag_adjoint: float32 [256, 256], replicated, may hold values from -6 to 6
Outputs:
- panel_grad: float32 [24576, 256], P(('row', 'col'))
- diag_grad: float32 [256, 256], replicated
Inputs may be any that keep to these rules, and one draw needn't show every extreme that they name: diag_factor is lower triangular with a diagonal between 1 and 2, and diag_inverse is its inverse. diag_factor is lower triangular with a diagonal between 1 and 2.
All inputs are finite; a program needn't handle non-finite values.
Results may differ from a plain program's by a relative error of at most 0.000057.
Values sent between devices are 32-bit elements; how exact they have to be, the bound alone decides.
A program may use at most 128 MiB of HBM per device.

v0:
```python
import jax
import jax.numpy as jnp
from jax import lax
from jax.sharding import PartitionSpec as P


def lower_half(matrix):
    return jnp.tril(matrix) - 0.5 * jnp.diag(jnp.diag(matrix))


def on_device(trail_adjoint, panel, panel_adjoint, diag_factor, diag_inverse, diag_adjoint):
    highest = lax.Precision.HIGHEST
    col_place = lax.axis_index("col")
    trail_width = trail_adjoint.shape[1]
    row_block = lax.all_gather(panel, "col", axis=0, tiled=True)
    full_panel = lax.all_gather(row_block, "row", axis=0, tiled=True)
    column_panel = lax.dynamic_slice_in_dim(full_panel, col_place * trail_width, trail_width, 0)
    image = lax.psum_scatter(
        jnp.dot(trail_adjoint, column_panel, precision=highest, preferred_element_type=jnp.float32),
        "col",
        scatter_dimension=0,
        tiled=True,
    )
    updated = panel_adjoint - 2.0 * image
    panel_grad = jnp.dot(
        updated, diag_inverse, precision=highest, preferred_element_type=jnp.float32
    )
    local_gram = jnp.dot(panel_grad.T, panel, precision=highest, preferred_element_type=jnp.float32)
    gram = lax.psum(local_gram, ("row", "col"))
    corner = diag_adjoint - gram
    inner = lower_half(
        jnp.dot(diag_factor.T, corner, precision=highest, preferred_element_type=jnp.float32)
    )
    left_part = jnp.dot(
        diag_inverse.T, inner, precision=highest, preferred_element_type=jnp.float32
    )
    diag_grad = lower_half(
        jnp.dot(left_part, diag_inverse, precision=highest, preferred_element_type=jnp.float32)
    )
    return (panel_grad, diag_grad)


def solution(mesh):
    in_specs = (P("row", "col"), P(("row", "col"), None), P(("row", "col"), None), P(), P(), P())
    out_specs = (P(("row", "col"), None), P())
    return jax.shard_map(
        on_device, mesh=mesh, in_specs=in_specs, out_specs=out_specs, check_vma=False
    )
```

profile of v0, /device:TPU:2, one launch (start us, length us, event | category | flops | bytes accessed | tf_op | source)
XLA Modules:
  0.0 522.4 jit_solution(10304371956958443014)
XLA Ops:
  7.2 0.0 copy-start
  7.2 0.0 copy-start.1
  7.2 0.0 copy-start.5
  7.2 0.0 copy-start.3
  7.2 0.0 copy-start.4
  7.2 0.0 all-gather.2.cloned.1.call-start
  7.3 14.9 %all_gather.6 = f32[768,256]{1,0:T(8,128)} all-gather(f32[96,256]{1,0:T(8,128)} %param.7), channel_id=1, replica_groups=mesh['row'=32,'col'=8] {'col'}, dimensions={0}, use_global_device_ids=true | all-gather | bytes 884736 | tf_op jit(solution)/shard_map/all_gather | solution.py:15
  22.1 0.0 all-gather.2.cloned.1.call-update
  22.2 0.0 reduce-scatter.2.cloned.1.call-start
  22.2 186.5 %all-gather.2.cloned.1.call-done = f32[24576,256]{1,0:T(8,128)} async-done(((f32[768,256]{1,0:T(8,128)}), f32[24576,256]{1,0:T(8,128)}) %all-gather.2.cloned.1.call-update) | async-done | bytes 25165840 | tf_op jit(solution)/shard_map/all_gather | solution.py:16
  208.7 11.5 %fusion.2 = f32[768,256]{1,0:T(8,128)} fusion(f32[768,3072]{1,0:T(8,128)} %param.6, f32[24576,256]{1,0:T(8,128)} %all-gather.2.cloned.1.call-done, s32[]{:T(128)S(6)} %select_n.26), kind=kOutput, calls=%fused_computation.4 | convolution fusion | flops 7247757312 | bytes 13369348 | tf_op jit(solution)/shard_map/dot_general | solution.py:19
  220.2 0.0 reduce-scatter.2.cloned.1.call-update
  220.3 0.0 all-reduce.2.cloned.1.call-start
  220.3 28.0 %reduce-scatter.2.cloned.1.call-done = f32[96,256]{1,0:T(8,128)} async-done(((f32[768,256]{1,0:T(8,128)}), f32[96,256]{1,0:T(8,128)}) %reduce-scatter.2.cloned.1.call-update) | async-done | bytes 98320 | tf_op jit(solution)/shard_map/reduce_scatter | solution.py:18
  248.3 0.0 copy-done
  248.3 0.0 copy-done.5
  248.3 1.2 fusion.14
  249.5 0.0 copy-done.1
  249.5 0.0 copy-start.2
  249.5 1.1 fusion.22
  250.6 0.0 all-reduce.2.cloned.1.call-update
  250.6 256.9 %all-reduce.2.cloned.1.call-done = f32[256,256]{1,0:T(8,128)} async-done(((f32[256,256]{1,0:T(8,128)}), f32[256,256]{1,0:T(8,128)}) %all-reduce.2.cloned.1.call-update) | async-done | bytes 262160 | tf_op jit(solution)/shard_map/psum | solution.py:29
  507.6 0.0 copy-done.3
  507.6 0.0 copy-done.4
  507.6 1.5 convolution_bitcast_fusion
  509.2 2.4 gather_fusion
  511.5 0.4 fusion.5
  511.9 0.6 fusion.23
  512.5 0.1 copy.10
  512.7 2.3 gather_fusion.1
  515.1 0.8 copy.11
  515.9 0.0 copy-done.2
  (2 shorter events, 0.0 us)
Async XLA Ops:
  7.2 241.1 %copy-start = (f32[256,256]{1,0:T(8,128)S(1)}, f32[256,256]{1,0:T(8,128)}, u32[]{:S(2)}) copy-start(f32[256,256]{1,0:T(8,128)} %param.10) | copy-start | bytes 786436
  7.2 242.3 %copy-start.1 = (f32[96,256]{1,0:T(8,128)S(1)}, f32[96,256]{1,0:T(8,128)}, u32[]{:S(2)}) copy-start(f32[96,256]{1,0:T(8,128)} %param.7) | copy-start | bytes 294916
  7.2 241.1 %copy-start.5 = (f32[96,256]{1,0:T(8,128)S(1)}, f32[96,256]{1,0:T(8,128)}, u32[]{:S(2)}) copy-start(f32[96,256]{1,0:T(8,128)} %param.8) | copy-start | bytes 294916
  7.2 500.4 %copy-start.3 = (f32[256,256]{1,0:T(8,128)S(1)}, f32[256,256]{1,0:T(8,128)}, u32[]{:S(2)}) copy-start(f32[256,256]{1,0:T(8,128)} %param.9) | copy-start | bytes 786436
  7.2 500.4 %copy-start.4 = (f32[256,256]{1,0:T(8,128)S(1)}, f32[256,256]{1,0:T(8,128)}, u32[]{:S(2)}) copy-start(f32[256,256]{1,0:T(8,128)} %param.11) | copy-start | bytes 786436
  7.2 201.5 %all-gather.2.cloned.1.call-start = ((), (), s32[]{:S(2)}) async-start(), calls=%async_computation.1 | async-start | bytes 25952256 | tf_op jit(solution)/shard_map/all_gather | solution.py:16
  22.2 226.1 %reduce-scatter.2.cloned.1.call-start = ((), (), s32[]{:S(2)}) async-start(), calls=%async_computation.2 | async-start | bytes 884736 | tf_op jit(solution)/shard_map/reduce_scatter | solution.py:18
  220.3 287.3 %all-reduce.2.cloned.1.call-start = ((), (), s32[]{:S(2)}) async-start(), calls=%async_computation.3 | async-start | bytes 524288 | tf_op jit(solution)/shard_map/psum | solution.py:29
  249.5 266.4 %copy-start.2 = (f32[96,256]{1,0:T(8,128)}, f32[96,256]{1,0:T(8,128)S(1)}, u32[]{:S(2)}) copy-start(f32[96,256]{1,0:T(8,128)S(1)} %fusion.14) | copy-start | bytes 294916
Sparse Core Ops, SparseCore 0:
  22.3 186.4 all-gather.1
  220.4 27.8 reduce-scatter.1
  255.2 252.3 all-reduce.1
where the time goes:
time: 523 us; the launch traced here: 522 us
  waiting for transfers between devices  472 us (90%)
  matrix products  16.3 us (3%)
  blocking collectives  14.9 us (3%)
  between operations  13.9 us (3%)
  local copies, waits for them, and re-layouts  5.71 us (1%)
    psum x1, waiting for transfers between devices, on_device(): gram = lax.psum(local_gram, ('row', 'col'))  257 us
    all_gather x1, waiting for transfers between devices, on_device(): full_panel = lax.all_gather(row_block, 'row', axis=0, tiled=True)  187 us
    reduce_scatter x1, waiting for transfers between devices, on_device(): lax.psum_scatter(jnp.dot(trail_adjoint, column_panel, precision=highest,...  28 us
    all_gather x1, blocking collectives, on_device(): row_block = lax.all_gather(panel, 'col', axis=0, tiled=True)  14.9 us
    dot_general x1, matrix products, on_device(): jnp.dot(trail_adjoint, column_panel, precision=highest, preferred_element...  11.5 us
  transfers between devices with their start and end apart: 3, of which 3 were waited for; matrix products, arithmetic and copies ran while one was open for 0% of the time, Pallas kernels for 0%

commit v1 on v0

--- a/solution.py
+++ b/solution.py
@@ -26,7 +26,7 @@
         updated, diag_inverse, precision=highest, preferred_element_type=jnp.float32
     )
     local_gram = jnp.dot(panel_grad.T, panel, precision=highest, preferred_element_type=jnp.float32)
-    gram = lax.psum(local_gram, ("row", "col"))
+    gram = lax.psum(lax.psum(local_gram, "col"), "row")
     corner = diag_adjoint - gram
     inner = lower_half(
         jnp.dot(diag_factor.T, corner, precision=highest, preferred_element_type=jnp.float32)

time: 523 us -> 480 us (0.918)
  waiting for transfers between devices: 472 us -> 429 us
    psum x1 -> x2, waiting for transfers between devices: 257 us -> 214 us  [on_device(): gram = lax.psum(lax.psum(local_gram, 'col'), 'row')]
  transfers between devices with their start and end apart: 3 -> 4, of which waited for: 3 -> 4; matrix products, arithmetic and copies ran while one was open for 0% -> 0% of each run, Pallas kernels for 0% -> 0%
where the time goes in v1:
time: 480 us
  waiting for transfers between devices  429 us (89%)
  matrix products  16.3 us (3%)
  blocking collectives  14.9 us (3%)
  between operations  13.9 us (3%)
  local copies, waits for them, and re-layouts  5.71 us (1%)
    psum x2, waiting for transfers between devices, on_device(): gram = lax.psum(lax.psum(local_gram, 'col'), 'row')  214 us
    all_gather x1, waiting for transfers between devices, on_device(): full_panel = lax.all_gather(row_block, 'row', axis=0, tiled=True)  187 us
    reduce_scatter x1, waiting for transfers between devices, on_device(): lax.psum_scatter(jnp.dot(trail_adjoint, column_panel, precision=highest,...  28 us
    all_gather x1, blocking collectives, on_device(): row_block = lax.all_gather(panel, 'col', axis=0, tiled=True)  14.9 us
    dot_general x1, matrix products, on_device(): jnp.dot(trail_adjoint, column_panel, precision=highest, preferred_element...  11.5 us
  transfers between devices with their start and end apart: 4, of which 4 were waited for; matrix products, arithmetic and copies ran while one was open for 0% of the time, Pallas kernels for 0%

profile of v1, /device:TPU:2, one launch (start us, length us, event | category | flops | bytes accessed | tf_op | source)
XLA Modules:
  0.0 479.7 jit_solution(7794428776500615939)
XLA Ops:
  7.2 0.0 copy-start
  7.2 0.0 copy-start.1
  7.2 0.0 copy-start.5
  7.2 0.0 copy-start.3
  7.2 0.0 copy-start.4
  7.2 0.0 all-gather.2.cloned.1.call-start
  7.3 14.9 %all_gather.6 = f32[768,256]{1,0:T(8,128)} all-gather(f32[96,256]{1,0:T(8,128)} %param.7), channel_id=1, replica_groups=mesh['row'=32,'col'=8] {'col'}, dimensions={0}, use_global_device_ids=true | all-gather | bytes 884736 | tf_op jit(solution)/shard_map/all_gather | solution.py:15
  22.1 0.0 all-gather.2.cloned.1.call-update
  22.2 0.0 reduce-scatter.2.cloned.1.call-start
  22.2 186.5 %all-gather.2.cloned.1.call-done = f32[24576,256]{1,0:T(8,128)} async-done(((f32[768,256]{1,0:T(8,128)}), f32[24576,256]{1,0:T(8,128)}) %all-gather.2.cloned.1.call-update) | async-done | bytes 25165840 | tf_op jit(solution)/shard_map/all_gather | solution.py:16
  208.7 11.5 %fusion.2 = f32[768,256]{1,0:T(8,128)} fusion(f32[768,3072]{1,0:T(8,128)} %param.6, f32[24576,256]{1,0:T(8,128)} %all-gather.2.cloned.1.call-done, s32[]{:T(128)S(6)} %select_n.26), kind=kOutput, calls=%fused_computation.4 | convolution fusion | flops 7247757312 | bytes 13369348 | tf_op jit(solution)/shard_map/dot_general | solution.py:19
  220.2 0.0 reduce-scatter.2.cloned.1.call-update
  220.3 0.0 all-reduce.3.cloned.1.call-start
  220.3 28.0 %reduce-scatter.2.cloned.1.call-done = f32[96,256]{1,0:T(8,128)} async-done(((f32[768,256]{1,0:T(8,128)}), f32[96,256]{1,0:T(8,128)}) %reduce-scatter.2.cloned.1.call-update) | async-done | bytes 98320 | tf_op jit(solution)/shard_map/reduce_scatter | solution.py:18
  248.3 0.0 copy-done
  248.3 0.0 copy-done.5
  248.3 1.2 fusion.14
  249.5 0.0 copy-start.2
  249.5 1.1 fusion.22
  250.6 0.0 all-reduce.3.cloned.1.call-update
  250.6 0.0 all-reduce.5.cloned.1.call-start
  250.7 65.3 %all-reduce.3.cloned.1.call-done = f32[256,256]{1,0:T(8,128)} async-done(((f32[256,256]{1,0:T(8,128)}), f32[256,256]{1,0:T(8,128)}) %all-reduce.3.cloned.1.call-update) | async-done | bytes 262160 | tf_op jit(solution)/shard_map/psum | solution.py:29
  316.0 0.0 all-reduce.5.cloned.1.call-update
  316.0 148.8 %all-reduce.5.cloned.1.call-done = f32[256,256]{1,0:T(8,128)} async-done(((f32[256,256]{1,0:T(8,128)}), f32[256,256]{1,0:T(8,128)}) %all-reduce.5.cloned.1.call-update) | async-done | bytes 262160 | tf_op jit(solution)/shard_map/psum | solution.py:29
  464.9 0.0 copy-done.3
  464.9 1.5 convolution_bitcast_fusion
  466.4 2.4 gather_fusion
  468.8 0.4 fusion.5
  469.2 0.6 fusion.23
  469.8 0.1 copy.10
  469.9 2.3 gather_fusion.1
  472.3 0.8 copy.11
  (5 shorter events, 0.1 us)
Async XLA Ops:
  7.2 241.1 %copy-start = (f32[256,256]{1,0:T(8,128)S(1)}, f32[256,256]{1,0:T(8,128)}, u32[]{:S(2)}) copy-start(f32[256,256]{1,0:T(8,128)} %param.10) | copy-start | bytes 786436
  7.2 242.3 %copy-start.1 = (f32[96,256]{1,0:T(8,128)S(1)}, f32[96,256]{1,0:T(8,128)}, u32[]{:S(2)}) copy-start(f32[96,256]{1,0:T(8,128)} %param.7) | copy-start | bytes 294916
  7.2 241.1 %copy-start.5 = (f32[96,256]{1,0:T(8,128)S(1)}, f32[96,256]{1,0:T(8,128)}, u32[]{:S(2)}) copy-start(f32[96,256]{1,0:T(8,128)} %param.8) | copy-start | bytes 294916
  7.2 457.7 %copy-start.3 = (f32[256,256]{1,0:T(8,128)S(1)}, f32[256,256]{1,0:T(8,128)}, u32[]{:S(2)}) copy-start(f32[256,256]{1,0:T(8,128)} %param.9) | copy-start | bytes 786436
  7.2 457.6 %copy-start.4 = (f32[256,256]{1,0:T(8,128)S(1)}, f32[256,256]{1,0:T(8,128)}, u32[]{:S(2)}) copy-start(f32[256,256]{1,0:T(8,128)} %param.11) | copy-start | bytes 786436
  7.2 201.5 %all-gather.2.cloned.1.call-start = ((), (), s32[]{:S(2)}) async-start(), calls=%async_computation.1 | async-start | bytes 25952256 | tf_op jit(solution)/shard_map/all_gather | solution.py:16
  22.2 226.1 %reduce-scatter.2.cloned.1.call-start = ((), (), s32[]{:S(2)}) async-start(), calls=%async_computation.2 | async-start | bytes 884736 | tf_op jit(solution)/shard_map/reduce_scatter | solution.py:18
  220.3 95.8 %all-reduce.3.cloned.1.call-start = ((), (), s32[]{:S(2)}) async-start(), calls=%async_computation.3 | async-start | bytes 524288 | tf_op jit(solution)/shard_map/psum | solution.py:29
  249.5 223.7 %copy-start.2 = (f32[96,256]{1,0:T(8,128)}, f32[96,256]{1,0:T(8,128)S(1)}, u32[]{:S(2)}) copy-start(f32[96,256]{1,0:T(8,128)S(1)} %fusion.14) | copy-start | bytes 294916
  250.6 214.2 %all-reduce.5.cloned.1.call-start = ((), (), s32[]{:S(2)}) async-start(), calls=%async_computation.4 | async-start | bytes 524288 | tf_op jit(solution)/shard_map/psum | solution.py:29
Sparse Core Ops, SparseCore 0:
  22.3 186.4 all-gather.1
  220.4 27.8 reduce-scatter.1
  251.3 64.6 all-reduce.2
  319.3 145.4 all-reduce.4
